TPU v7x, 128 devices: a whole 4x4x4 slice. The times are simulated.
128 devices in a mesh: row: 8 (over x, core), col: 16 (over z, y).
Axes of the slice: x: 4, y: 4, z: 4, core: 2. Of those that a mesh axis runs over, the one named last changes fastest.
Arguments:
- observed: bfloat16 [4096, 8, 128, 128], P(('row', 'col')), may hold values from -6 to 6
- sku_ids: int32 [4096], P(('row', 'col')), may hold values from 0 to 15
- store_ids: int32 [4096, 8], P(('row', 'col')), may hold values from 0 to 79
- live_slot_counts: int32 [8, 16, 8], P('row', 'col'), may hold values from 0 to 4, as said below
- sku_factors: float32 [262144, 256], P(('row', 'col')), may hold values from -1.5 to 1.5
- store_factors: float32 [81920, 256], P(('row', 'col')), may hold values from -1.5 to 1.5
Outputs:
- new_sku_factors: float32 [262144, 256], P(('row', 'col'))
- new_store_factors: float32 [81920, 256], P(('row', 'col'))
Inputs may be any that keep to these rules, and one draw needn't show every extreme that they name: `live_slot_counts`: in every column index some owner row's slots are full from every device of that column.
All inputs are finite; a program needn't handle non-finite values.
Results may differ from a plain program's by a relative error of at most 0.023.
Values may be sent and summed in bfloat16 or wider, within the bound.
A program may use at most 192 MiB of HBM per device.

v0:
```python
import jax
import jax.numpy as jnp
from jax import lax
from jax.sharding import PartitionSpec as P

learn_rate = 0.01
weight_decay = 0.05
group_rows = 8


def one_hot_of(ids, count):
    return (
        ids[..., None] == lax.broadcasted_iota(jnp.int32, ids.shape + (count,), ids.ndim)
    ).astype(jnp.bfloat16)


def pick_blocks(table, ids):
    selector = one_hot_of(ids.reshape(-1), table.shape[0])
    flat_table = table.reshape(table.shape[0], -1)
    picked = jnp.dot(selector, flat_table, preferred_element_type=jnp.float32).astype(jnp.bfloat16)
    return picked.reshape(ids.shape + table.shape[1:])


def sum_into_blocks(selector, values):
    flat_values = values.reshape(values.shape[0], -1)
    high_part = flat_values.astype(jnp.bfloat16)
    low_part = (flat_values - high_part.astype(jnp.float32)).astype(jnp.bfloat16)
    upper = jnp.einsum("nv,nx->vx", selector, high_part, preferred_element_type=jnp.float32)
    lower = jnp.einsum("nv,nx->vx", selector, low_part, preferred_element_type=jnp.float32)
    return upper + lower


def local(observed, sku_ids, store_ids, live_slot_counts, sku_factors, store_factors):
    rows_per_owner = lax.axis_size("row")
    total_live_slots = observed.shape[0]
    owner_wise = total_live_slots // rows_per_owner
    block_len = observed.shape[2]
    rank_len = sku_factors.shape[1]
    slot_alive_mask = lax.broadcasted_iota(
        jnp.int32, (rows_per_owner, owner_wise), 1
    ) < live_slot_counts.reshape(rows_per_owner, 1)
    slot_alive_mask = slot_alive_mask.reshape(total_live_slots).astype(jnp.float32)
    own_sku = sku_factors.reshape(-1, block_len, rank_len)
    own_table = own_sku.astype(jnp.bfloat16)
    own_store = store_factors.reshape(-1, block_len, rank_len)
    requested_ids = sku_ids.reshape(rows_per_owner, owner_wise)
    all_tables = lax.all_gather(own_table, "row", axis=0, tiled=True)
    owner_row = jnp.arange(total_live_slots, dtype=jnp.int32) // owner_wise
    fetched = pick_blocks(all_tables, owner_row * own_table.shape[0] + sku_ids)
    group_low = lax.all_gather(own_store.astype(jnp.bfloat16), "col", axis=0, tiled=True)
    group_count = group_low.shape[0]
    count_groups = total_live_slots // group_rows

    def split_into_groups(array_in):
        return array_in.reshape((count_groups, group_rows) + array_in.shape[1:])

    input_arrays = (
        split_into_groups(fetched),
        split_into_groups(observed),
        split_into_groups(store_ids),
        split_into_groups(slot_alive_mask),
    )

    def misfit_of(factor_rows, measured, store_pick, store_table):
        selected = pick_blocks(store_table, store_pick)
        predicted = jnp.einsum(
            "sar,skbr->skab", factor_rows, selected, preferred_element_type=jnp.float32
        )
        misfit = (predicted - measured.astype(jnp.float32)).astype(jnp.bfloat16)
        return (misfit, selected)

    def first_pass(running, inputs_now):
        factor_rows, measured, store_pick, alive = inputs_now
        misfit, selected = misfit_of(factor_rows, measured, store_pick, group_low)
        partial_value = jnp.einsum(
            "skab,sar->skbr", misfit, factor_rows, preferred_element_type=jnp.float32
        )
        selector = one_hot_of(store_pick, group_count) * alive[:, None, None].astype(jnp.bfloat16)
        selector = selector.reshape(-1, group_count)
        added = sum_into_blocks(selector, partial_value.reshape(-1, block_len, rank_len))
        return (running + added.reshape(running.shape), None)

    store_grad, _ = lax.scan(first_pass, jnp.zeros(group_low.shape, jnp.float32), input_arrays)
    own_grad = lax.psum_scatter(
        store_grad.astype(jnp.bfloat16), "col", scatter_dimension=0, tiled=True
    ).astype(jnp.float32)
    new_store = own_store - learn_rate * (own_grad + weight_decay * own_store)
    new_low = lax.all_gather(new_store.astype(jnp.bfloat16), "col", axis=0, tiled=True)

    def second_pass(running, inputs_now):
        factor_rows, measured, store_pick, alive = inputs_now
        misfit, selected = misfit_of(factor_rows, measured, store_pick, new_low)
        partial_value = jnp.einsum(
            "skab,skbr->sar", misfit, selected, preferred_element_type=jnp.float32
        )
        return (running, partial_value * alive[:, None, None])

    _, sku_terms = lax.scan(second_pass, jnp.zeros((), jnp.float32), input_arrays)
    sku_terms = sku_terms.reshape(rows_per_owner, owner_wise, block_len, rank_len)
    arrived, requested = (
        lax.all_to_all(
            sku_terms.astype(jnp.bfloat16), "row", split_axis=0, concat_axis=0, tiled=True
        ).astype(sku_terms.dtype),
        lax.all_to_all(requested_ids, "row", split_axis=0, concat_axis=0, tiled=True),
    )
    owner_selector = one_hot_of(requested.reshape(-1), own_sku.shape[0])
    sku_grad = sum_into_blocks(owner_selector, arrived.reshape(-1, block_len, rank_len)).reshape(
        own_sku.shape
    )
    new_sku = own_sku - learn_rate * (sku_grad + weight_decay * own_sku)
    return (new_sku.reshape(sku_factors.shape), new_store.reshape(store_factors.shape))


def solution(mesh):
    placed = (
        P(("row", "col"), None, None, None),
        P(("row", "col")),
        P(("row", "col"), None),
        P("row", "col", None),
        P(("row", "col"), None),
        P(("row", "col"), None),
    )
    return jax.shard_map(
        local,
        mesh=mesh,
        in_specs=placed,
        out_specs=(P(("row", "col"), None), P(("row", "col"), None)),
        check_vma=False,
    )
```

profile of v0, /device:TPU:1, one launch (start us, length us, event | category | flops | bytes accessed | tf_op | source)
XLA Modules:
  0.0 615.1 jit_solution(6437054069210750327)
XLA Ops:
  12.4 12.0 %copy.26 = bf16[32,8,128,128]{2,3,1,0:T(8,128)(2,1)} copy(bf16[32,8,128,128]{3,2,1,0:T(8,128)(2,1)} %param.10) | data formatting | bytes 16777216 | tf_op args[0]
  25.1 38.6 %all-gather.6.cloned.1.call-done = bf16[128,128,256]{2,1,0:T(8,128)(2,1)} async-done(((bf16[16,128,256]{2,1,0:T(8,128)(2,1)}), bf16[128,128,256]{2,1,0:T(8,128)(2,1)}) %all-gather.6.cloned.1.call-update) | async-done | bytes 8388624 | tf_op jit(solution)/shard_map/all_gather | solution.py:47
  63.7 12.3 %copy.38 = bf16[16,8,128,256]{3,1,2,0:T(8,128)(2,1)} copy(bf16[16,8,128,256]{3,2,1,0:T(8,128)(2,1)} %bitcast.187) | data formatting | bytes 16777216
  81.3 41.4 %all-gather.4.cloned.1.call-done = bf16[80,128,256]{2,1,0:T(8,128)(2,1)} async-done(((bf16[5,128,256]{2,1,0:T(8,128)(2,1)}), bf16[80,128,256]{2,1,0:T(8,128)(2,1)}) %all-gather.4.cloned.1.call-update) | async-done | bytes 5242896 | tf_op jit(solution)/shard_map/all_gather | solution.py:50
  122.7 230.6 %while.22 = (s32[]{:T(128)}, f32[80,128,256]{2,1,0:T(8,128)}, s32[4,8,8]{2,1,0:T(8,128)S(1)}, bf16[4,8]{1,0:T(4,128)(2,1)S(1)}, bf16[80,128,256]{2,1,0:T(8,128)(...) while((s32[]{:T(128)}, f32[80,128,256]{2,1,0:T(8,128)}, ...), condition=%wide.region_1.2_spmd.clone, body=%wide.region_0.1_spmd.clone.sunk | while | flops 2101896192 | bytes 161484752 | solution.py:83
  137.1 5.8 copy.84
  146.3 8.8 %fusion.141 = (bf16[8,8,128,256]{3,2,1,0:T(8,128)(2,1)}, bf16[8,8,128,256]{3,2,1,0:T(8,128)(2,1)}) fusion(bf16[4,8,128,256]{3,2,1,0:T(8,128)(2,1)S(1)} %get-tuple-element.291, s32[]{:T(128)} %get-tuple-element.277, bf16[8,8,128,256]{3,1,2,0:T(8,128)(2,1)} %bitcast.177, bf16[4,8,8,128,128]{3,4,2,1,0:T(8,128)(2,1)} %get-tuple-element.292), kind=kOutput, calls=%fused_computation.25.clone.1 | convolution fusion | flops 1085276160 | bytes 15730176 | tf_op jit(solution)/shard_map/while/body/eval_jaxpr/skab,sar->skbr/dot_general | solution.py:75
  170.6 7.1 %copy.87 = f32[10,8,128,256]{3,2,1,0:T(8,128)} copy(f32[10,8,128,256]{3,1,2,0:T(8,128)S(1)} %bitcast.174) | data formatting | bytes 20971520 | tf_op jit(solution)/shard_map/while
  177.7 11.1 %bitcast_add_fusion.2 = f32[80,128,256]{2,1,0:T(8,128)} fusion(f32[10,8,128,256]{3,2,1,0:T(8,128)} %copy.87, f32[80,128,256]{2,1,0:T(8,128)} %get-tuple-element.278, pred[]{:T(512)S(6)} %compare.5), kind=kLoop, calls=%fused_computation.23.clone.1 | loop fusion | flops 5242880 | bytes 31457280 | tf_op jit(solution)/shard_map/while/body/eval_jaxpr/add | solution.py:81
  189.0 5.8 copy.84
  198.1 8.8 %fusion.141 = (bf16[8,8,128,256]{3,2,1,0:T(8,128)(2,1)}, bf16[8,8,128,256]{3,2,1,0:T(8,128)(2,1)}) fusion(bf16[4,8,128,256]{3,2,1,0:T(8,128)(2,1)S(1)} %get-tuple-element.291, s32[]{:T(128)} %get-tuple-element.277, bf16[8,8,128,256]{3,1,2,0:T(8,128)(2,1)} %bitcast.177, bf16[4,8,8,128,128]{3,4,2,1,0:T(8,128)(2,1)} %get-tuple-element.292), kind=kOutput, calls=%fused_computation.25.clone.1 | convolution fusion | flops 1085276160 | bytes 15730176 | tf_op jit(solution)/shard_map/while/body/eval_jaxpr/skab,sar->skbr/dot_general | solution.py:75
  222.4 7.1 %copy.87 = f32[10,8,128,256]{3,2,1,0:T(8,128)} copy(f32[10,8,128,256]{3,1,2,0:T(8,128)S(1)} %bitcast.174) | data formatting | bytes 20971520 | tf_op jit(solution)/shard_map/while
  229.5 14.1 %bitcast_add_fusion.2 = f32[80,128,256]{2,1,0:T(8,128)} fusion(f32[10,8,128,256]{3,2,1,0:T(8,128)} %copy.87, f32[80,128,256]{2,1,0:T(8,128)} %get-tuple-element.278, pred[]{:T(512)S(6)} %compare.5), kind=kLoop, calls=%fused_computation.23.clone.1 | loop fusion | flops 5242880 | bytes 31457280 | tf_op jit(solution)/shard_map/while/body/eval_jaxpr/add | solution.py:81
  243.7 5.8 copy.84
  252.9 8.8 %fusion.141 = (bf16[8,8,128,256]{3,2,1,0:T(8,128)(2,1)}, bf16[8,8,128,256]{3,2,1,0:T(8,128)(2,1)}) fusion(bf16[4,8,128,256]{3,2,1,0:T(8,128)(2,1)S(1)} %get-tuple-element.291, s32[]{:T(128)} %get-tuple-element.277, bf16[8,8,128,256]{3,1,2,0:T(8,128)(2,1)} %bitcast.177, bf16[4,8,8,128,128]{3,4,2,1,0:T(8,128)(2,1)} %get-tuple-element.292), kind=kOutput, calls=%fused_computation.25.clone.1 | convolution fusion | flops 1085276160 | bytes 15730176 | tf_op jit(solution)/shard_map/while/body/eval_jaxpr/skab,sar->skbr/dot_general | solution.py:75
  277.2 7.1 %copy.87 = f32[10,8,128,256]{3,2,1,0:T(8,128)} copy(f32[10,8,128,256]{3,1,2,0:T(8,128)S(1)} %bitcast.174) | data formatting | bytes 20971520 | tf_op jit(solution)/shard_map/while
  284.3 14.1 %bitcast_add_fusion.2 = f32[80,128,256]{2,1,0:T(8,128)} fusion(f32[10,8,128,256]{3,2,1,0:T(8,128)} %copy.87, f32[80,128,256]{2,1,0:T(8,128)} %get-tuple-element.278, pred[]{:T(512)S(6)} %compare.5), kind=kLoop, calls=%fused_computation.23.clone.1 | loop fusion | flops 5242880 | bytes 31457280 | tf_op jit(solution)/shard_map/while/body/eval_jaxpr/add | solution.py:81
  298.5 5.8 copy.84
  307.7 8.8 %fusion.141 = (bf16[8,8,128,256]{3,2,1,0:T(8,128)(2,1)}, bf16[8,8,128,256]{3,2,1,0:T(8,128)(2,1)}) fusion(bf16[4,8,128,256]{3,2,1,0:T(8,128)(2,1)S(1)} %get-tuple-element.291, s32[]{:T(128)} %get-tuple-element.277, bf16[8,8,128,256]{3,1,2,0:T(8,128)(2,1)} %bitcast.177, bf16[4,8,8,128,128]{3,4,2,1,0:T(8,128)(2,1)} %get-tuple-element.292), kind=kOutput, calls=%fused_computation.25.clone.1 | convolution fusion | flops 1085276160 | bytes 15730176 | tf_op jit(solution)/shard_map/while/body/eval_jaxpr/skab,sar->skbr/dot_general | solution.py:75
  332.0 7.1 %copy.87 = f32[10,8,128,256]{3,2,1,0:T(8,128)} copy(f32[10,8,128,256]{3,1,2,0:T(8,128)S(1)} %bitcast.174) | data formatting | bytes 20971520 | tf_op jit(solution)/shard_map/while
  339.1 14.1 %bitcast_add_fusion.2 = f32[80,128,256]{2,1,0:T(8,128)} fusion(f32[10,8,128,256]{3,2,1,0:T(8,128)} %copy.87, f32[80,128,256]{2,1,0:T(8,128)} %get-tuple-element.278, pred[]{:T(512)S(6)} %compare.5), kind=kLoop, calls=%fused_computation.23.clone.1 | loop fusion | flops 5242880 | bytes 31457280 | tf_op jit(solution)/shard_map/while/body/eval_jaxpr/add | solution.py:81
  353.2 7.1 %convert_element_type.99 = bf16[80,128,256]{2,1,0:T(8,128)(2,1)} convert(f32[80,128,256]{2,1,0:T(8,128)} %get-tuple-element.76) | non-fusion elementwise | flops 2621440 | bytes 15728640 | tf_op jit(solution)/shard_map/convert_element_type | solution.py:85
  360.4 78.1 %reduce-scatter.4.cloned.1.call-done = bf16[5,128,256]{2,1,0:T(8,128)(2,1)} async-done(((bf16[80,128,256]{2,1,0:T(8,128)(2,1)}), bf16[5,128,256]{2,1,0:T(8,128)(2,1)}) %reduce-scatter.4.cloned.1.call-update) | async-done | bytes 327696
  441.2 6.0 all-to-all-start
  447.2 50.2 %all-gather.8.cloned.1.call-done = bf16[80,128,256]{2,1,0:T(8,128)(2,1)} async-done(((bf16[5,128,256]{2,1,0:T(8,128)(2,1)}), bf16[80,128,256]{2,1,0:T(8,128)(2,1)}) %all-gather.8.cloned.1.call-update) | async-done | bytes 5242896 | tf_op jit(solution)/shard_map/all_gather | solution.py:88
  497.5 69.7 %while.21 = (s32[]{:T(128)}, bf16[4,8,128,256]{3,2,1,0:T(8,128)(2,1)}, s32[4,8,8]{2,1,0:T(8,128)S(1)}, bf16[80,128,256]{2,1,0:T(8,128)(2,1)}, bf16[4,8,128,256]{...) while((s32[]{:T(128)}, ...), condition=%wide.region_4.5_spmd, body=%wide.region_3.4_spmd.sunk | while | flops 1414796288 | bytes 31985052 | solution.py:98
  497.5 5.8 copy.82
  507.3 7.6 %fusion.131 = bf16[4,8,128,256]{3,2,1,0:T(8,128)(2,1)} fusion(bf16[4,8,128,256]{3,2,1,0:T(8,128)(2,1)} %get-tuple-element.304, s32[]{:T(128)} %get-tuple-element.303, bf16[8,8,128,256]{3,1,2,0:T(8,128)(2,1)} %bitcast.182, bf16[4,8,8,128,128]{3,4,2,1,0:T(8,128)(2,1)} %get-tuple-element.316, f32[8]{0:T(128)S(1)} %fusion.130, ...), kind=kOutput, calls=%fused_computation.12.clone.1 | convolution fusion | flops 1077149696 | bytes 12060672 | tf_op jit(solution)/shard_map/while/body/eval_jaxpr/skab,skbr->sar/dot_general | solution.py:93
  524.7 7.6 %fusion.131 = bf16[4,8,128,256]{3,2,1,0:T(8,128)(2,1)} fusion(bf16[4,8,128,256]{3,2,1,0:T(8,128)(2,1)} %get-tuple-element.304, s32[]{:T(128)} %get-tuple-element.303, bf16[8,8,128,256]{3,1,2,0:T(8,128)(2,1)} %bitcast.182, bf16[4,8,8,128,128]{3,4,2,1,0:T(8,128)(2,1)} %get-tuple-element.316, f32[8]{0:T(128)S(1)} %fusion.130, ...), kind=kOutput, calls=%fused_computation.12.clone.1 | convolution fusion | flops 1077149696 | bytes 12060672 | tf_op jit(solution)/shard_map/while/body/eval_jaxpr/skab,skbr->sar/dot_general | solution.py:93
  542.1 7.6 %fusion.131 = bf16[4,8,128,256]{3,2,1,0:T(8,128)(2,1)} fusion(bf16[4,8,128,256]{3,2,1,0:T(8,128)(2,1)} %get-tuple-element.304, s32[]{:T(128)} %get-tuple-element.303, bf16[8,8,128,256]{3,1,2,0:T(8,128)(2,1)} %bitcast.182, bf16[4,8,8,128,128]{3,4,2,1,0:T(8,128)(2,1)} %get-tuple-element.316, f32[8]{0:T(128)S(1)} %fusion.130, ...), kind=kOutput, calls=%fused_computation.12.clone.1 | convolution fusion | flops 1077149696 | bytes 12060672 | tf_op jit(solution)/shard_map/while/body/eval_jaxpr/skab,skbr->sar/dot_general | solution.py:93
  559.6 7.6 %fusion.131 = bf16[4,8,128,256]{3,2,1,0:T(8,128)(2,1)} fusion(bf16[4,8,128,256]{3,2,1,0:T(8,128)(2,1)} %get-tuple-element.304, s32[]{:T(128)} %get-tuple-element.303, bf16[8,8,128,256]{3,1,2,0:T(8,128)(2,1)} %bitcast.182, bf16[4,8,8,128,128]{3,4,2,1,0:T(8,128)(2,1)} %get-tuple-element.316, f32[8]{0:T(128)S(1)} %fusion.130, ...), kind=kOutput, calls=%fused_computation.12.clone.1 | convolution fusion | flops 1077149696 | bytes 12060672 | tf_op jit(solution)/shard_map/while/body/eval_jaxpr/skab,skbr->sar/dot_general | solution.py:93
  572.8 25.6 %all-to-all-done.1 = bf16[8,4,128,256]{3,2,1,0:T(8,128)(2,1)S(1)} async-done(((bf16[8,4,128,256]{3,2,1,0:T(8,128)(2,1)}), bf16[8,4,128,256]{3,2,1,0:T(8,128)(2,1)S(1)}, u32[]{:S(2)}, u32[]{:S(2)}) %all-to-all-start.1) | async-done | bytes 2097184 | tf_op jit(solution)/shard_map/all_to_all | solution.py:101
  (112 shorter events, 138.5 us)
Async XLA Ops:
  7.2 2.9 copy-start.2
  7.2 4.2 copy-start.7
  7.2 56.5 %all-gather.6.cloned.1.call-start = ((), (), s32[]{:S(2)}) async-start(), calls=%async_computation.4 | async-start | bytes 9437184 | tf_op jit(solution)/shard_map/all_gather | solution.py:47
  10.0 112.7 %all-gather.4.cloned.1.call-start = ((), (), s32[]{:S(2)}) async-start(), calls=%async_computation.3 | async-start | bytes 5570560 | tf_op jit(solution)/shard_map/all_gather | solution.py:50
  10.8 427.6 %reduce-scatter.4.cloned.1.call-start = ((), (), s32[]{:S(2)}) async-start(), calls=%async_computation.6 | async-start | bytes 5570560
  12.4 12.0 %copy-start.4 = (s32[32,8]{0,1:T(8,128)S(1)}, s32[32,8]{0,1:T(8,128)}, u32[]{:S(2)}) copy-start(s32[32,8]{0,1:T(8,128)} %param.12) | copy-start | bytes 3076
  12.4 12.1 %copy-start.5 = (s32[32]{0:T(128)S(1)}, s32[32]{0:T(128)}, u32[]{:S(2)}) copy-start(s32[32]{0:T(128)} %param.11) | copy-start | bytes 388
  159.9 2.2 copy-start
  211.7 2.2 copy-start
  266.5 2.2 copy-start
  321.3 2.2 copy-start
  360.3 78.2 %copy-start.3 = (f32[640,256]{1,0:T(8,128)S(1)}, f32[640,256]{1,0:T(8,128)}, u32[]{:S(2)}) copy-start(f32[640,256]{1,0:T(8,128)} %param.15) | copy-start | bytes 1966084
  360.3 80.2 %copy-start.6 = (s32[32]{0:T(128)S(1)}, s32[32]{0:T(128)}, u32[]{:S(2)}) copy-start(s32[32]{0:T(128)} %param.11) | copy-start | bytes 388
  360.3 137.1 %all-gather.8.cloned.1.call-start = ((), (), s32[]{:S(2)}) async-start(), calls=%async_computation.5 | async-start | bytes 5570560 | tf_op jit(solution)/shard_map/all_gather | solution.py:88
  441.2 126.0 %all-to-all-start = ((s32[8,1,4]{2,1,0:T(1,128)}), s32[8,1,4]{2,1,0:T(1,128)S(1)}, u32[]{:S(2)}, u32[]{:S(2)}) async-start(s32[8,1,4]{2,1,0:T(1,128)} %bitcast.10), calls=%async_computation | async-start | bytes 8192 | tf_op jit(solution)/shard_map/all_to_all | solution.py:104
  567.2 31.3 %all-to-all-start.1 = ((bf16[8,4,128,256]{3,2,1,0:T(8,128)(2,1)}), bf16[8,4,128,256]{3,2,1,0:T(8,128)(2,1)S(1)}, u32[]{:S(2)}, u32[]{:S(2)}) async-start(bf16[8,4,128,256]{3,2,1,0:T(8,128)(2,1)} %bitcast.193), calls=%async_computation.1 | async-start | bytes 4194304 | tf_op jit(solution)/shard_map/all_to_all | solution.py:101
  600.2 4.8 copy-start.1
Sparse Core Ops, SparseCore 0:
  10.3 53.3 all-gather.5
  66.4 56.2 all-gather.3
  360.5 77.9 reduce-scatter.3
  440.7 56.7 all-gather.7
where the time goes:
time: 623 us; the launch traced here: 615 us
  waiting for transfers between devices  234 us (38%)
  local copies, waits for them, and re-layouts  149 us (24%)
  matrix products  121 us (19%)
  other arithmetic  71.3 us (11%)
  loops' own time  14.6 us (2%)
  between operations  14.2 us (2%)
  starting transfers between devices  11.1 us (2%)
    while x28, local copies, waits for them, and re-layouts  115 us
    unnamed x5, waiting for transfers between devices  78.1 us
    add x4, other arithmetic, first_pass(): return (running + added.reshape(running.shape), None)  53.5 us
    all_gather x1, waiting for transfers between devices, local(): lax.all_gather(new_store.astype(jnp.bfloat16), 'col', axis=0, tiled=True)  50.2 us
    all_gather x1, waiting for transfers between devices, local(): lax.all_gather(own_store.astype(jnp.bfloat16), 'col', axis=0, tiled=True)  41.4 us
    all_gather x1, waiting for transfers between devices, local(): all_tables = lax.all_gather(own_table, 'row', axis=0, tiled=True)  38.6 us
    dot_general x4, matrix products, first_pass(): jnp.einsum('skab,sar->skbr', misfit, factor_rows, preferred_element_type=...  35.2 us
    dot_general x9, matrix products, pick_blocks(): jnp.dot(selector, flat_table, preferred_element_type=jnp.float32)  31.1 us
  transfers between devices with their start and end apart: 6, of which 5 were waited for; matrix products, arithmetic and copies ran while one was open for 17% of the time, Pallas kernels for 0%

commit v1 on v0

--- a/solution.py
+++ b/solution.py
@@ -6,6 +6,22 @@
 learn_rate = 0.01
 weight_decay = 0.05
 group_rows = 8
+
+
+def ring_gather(x, axis, dim):
+    ways, here, step = (lax.axis_size(axis), lax.axis_index(axis), x.shape[dim])
+    shape = [n * ways if d == dim else n for d, n in enumerate(x.shape)]
+    full = lax.dynamic_update_slice_in_dim(jnp.zeros(shape, x.dtype), x, here * step, axis=dim)
+    going_up = going_down = x
+    for far in range(1, ways // 2 + 1):
+        going_up = lax.ppermute(going_up, axis, [(d, (d + 1) % ways) for d in range(ways)])
+        full = lax.dynamic_update_slice_in_dim(full, going_up, (here - far) % ways * step, axis=dim)
+        if 2 * far < ways:
+            going_down = lax.ppermute(going_down, axis, [(d, (d - 1) % ways) for d in range(ways)])
+            full = lax.dynamic_update_slice_in_dim(
+                full, going_down, (here + far) % ways * step, axis=dim
+            )
+    return full
 
 
 def one_hot_of(ids, count):
@@ -85,7 +101,7 @@
         store_grad.astype(jnp.bfloat16), "col", scatter_dimension=0, tiled=True
     ).astype(jnp.float32)
     new_store = own_store - learn_rate * (own_grad + weight_decay * own_store)
-    new_low = lax.all_gather(new_store.astype(jnp.bfloat16), "col", axis=0, tiled=True)
+    new_low = ring_gather(new_store.astype(jnp.bfloat16), "col", 0)
 
     def second_pass(running, inputs_now):
         factor_rows, measured, store_pick, alive = inputs_now

time: 623 us -> 662 us (1.063)
  starting transfers between devices: 11.1 us -> 52.5 us
  waiting for transfers between devices: 234 us -> 215 us
  local copies, waits for them, and re-layouts: 149 us -> 166 us
    all_gather x1 -> x0, waiting for transfers between devices: 50.2 us -> none  [local(): lax.all_gather(new_store.astype(jnp.bfloat16), 'col', axis=0, tiled=True)]
    ppermute x0 -> x15, starting transfers between devices: none -> 36 us  [the longest x7 35 us: ring_gather(): lax.ppermute(going_down, axis, [(d, (d - 1) % ways) for d in range(ways)])]
    ppermute x0 -> x15, waiting for transfers between devices: none -> 32.8 us  [the longest x8 21.7 us: ring_gather(): lax.ppermute(going_up, axis, [(d, (d + 1) % ways) for d in range(ways)])]
    dynamic_update_slice x0 -> x15, local copies, waits for them, and re-layouts: none -> 14.2 us  [the longest x7 7.21 us: ring_gather(): lax.dynamic_update_slice_in_dim(full, going_down, (here + far) % ways * s...]
    unnamed x5 -> x4, waiting for transfers between devices: 78.1 us -> 77.8 us
    unnamed x20 -> x24, local copies, waits for them, and re-layouts: 26.7 us -> 26.7 us
  transfers between devices with their start and end apart: 6 -> 20, of which waited for: 5 -> 14; matrix products, arithmetic and copies ran while one was open for 17% -> 18% of each run, Pallas kernels for 0% -> 0%
where the time goes in v1:
time: 662 us; the launch traced here: 654 us
  waiting for transfers between devices  215 us (32%)
  local copies, waits for them, and re-layouts  166 us (25%)
  matrix products  121 us (18%)
  other arithmetic  71 us (11%)
  starting transfers between devices  52.5 us (8%)
  loops' own time  14.8 us (2%)
  between operations  14.1 us (2%)
    while x28, local copies, waits for them, and re-layouts  115 us
    unnamed x4, waiting for transfers between devices  77.8 us
    add x4, other arithmetic, first_pass(): return (running + added.reshape(running.shape), None)  53.4 us
    all_gather x1, waiting for transfers between devices, local(): lax.all_gather(own_store.astype(jnp.bfloat16), 'col', axis=0, tiled=True)  41.4 us
    all_gather x1, waiting for transfers between devices, local(): all_tables = lax.all_gather(own_table, 'row', axis=0, tiled=True)  37.7 us
    ppermute x7, starting transfers between devices, ring_gather(): lax.ppermute(going_down, axis, [(d, (d - 1) % ways) for d in range(ways)])  35 us
    dot_general x4, matrix products, first_pass(): jnp.einsum('skab,sar->skbr', misfit, factor_rows, preferred_element_type=...  34.7 us
    dot_general x9, matrix products, pick_blocks(): jnp.dot(selector, flat_table, preferred_element_type=jnp.float32)  31 us
  transfers between devices with their start and end apart: 20, of which 14 were waited for; matrix products, arithmetic and copies ran while one was open for 18% of the time, Pallas kernels for 0%

profile of v1, /device:TPU:1, one launch (start us, length us, event | category | flops | bytes accessed | tf_op | source)
XLA Modules:
  0.0 654.1 jit_solution(3171914817009419765)
XLA Ops:
  13.3 12.1 %copy.26 = bf16[32,8,128,128]{2,3,1,0:T(8,128)(2,1)} copy(bf16[32,8,128,128]{3,2,1,0:T(8,128)(2,1)} %param.10) | data formatting | bytes 16777216 | tf_op args[0]
  26.0 37.7 %all-gather.5.cloned.1.call-done = bf16[128,128,256]{2,1,0:T(8,128)(2,1)} async-done(((bf16[16,128,256]{2,1,0:T(8,128)(2,1)}), bf16[128,128,256]{2,1,0:T(8,128)(2,1)}) %all-gather.5.cloned.1.call-update) | async-done | bytes 8388624 | tf_op jit(solution)/shard_map/all_gather | solution.py:63
  63.6 12.3 %copy.38 = bf16[16,8,128,256]{3,1,2,0:T(8,128)(2,1)} copy(bf16[16,8,128,256]{3,2,1,0:T(8,128)(2,1)} %bitcast.186) | data formatting | bytes 16777216
  81.3 41.4 %all-gather.3.cloned.1.call-done = bf16[80,128,256]{2,1,0:T(8,128)(2,1)} async-done(((bf16[5,128,256]{2,1,0:T(8,128)(2,1)}), bf16[80,128,256]{2,1,0:T(8,128)(2,1)}) %all-gather.3.cloned.1.call-update) | async-done | bytes 5242896 | tf_op jit(solution)/shard_map/all_gather | solution.py:66
  122.6 229.7 %while.22 = (s32[]{:T(128)}, f32[80,128,256]{2,1,0:T(8,128)}, s32[4,8,8]{2,1,0:T(8,128)S(1)}, bf16[4,8]{1,0:T(4,128)(2,1)S(1)}, bf16[80,128,256]{2,1,0:T(8,128)(...) while((s32[]{:T(128)}, f32[80,128,256]{2,1,0:T(8,128)}, ...), condition=%wide.region_1.2_spmd.clone, body=%wide.region_0.1_spmd.clone.sunk | while | flops 2101896192 | bytes 161484752 | solution.py:99
  137.1 5.8 copy.84
  146.3 8.7 %fusion.140 = (bf16[8,8,128,256]{3,2,1,0:T(8,128)(2,1)}, bf16[8,8,128,256]{3,2,1,0:T(8,128)(2,1)}) fusion(bf16[4,8,128,256]{3,2,1,0:T(8,128)(2,1)S(1)} %get-tuple-element.292, s32[]{:T(128)} %get-tuple-element.278, bf16[8,8,128,256]{3,1,2,0:T(8,128)(2,1)} %bitcast.177, bf16[4,8,8,128,128]{3,4,2,1,0:T(8,128)(2,1)} %get-tuple-element.293), kind=kOutput, calls=%fused_computation.25.clone.1 | convolution fusion | flops 1085276160 | bytes 15730176 | tf_op jit(solution)/shard_map/while/body/eval_jaxpr/skab,sar->skbr/dot_general | solution.py:91
  170.5 7.1 %copy.87 = f32[10,8,128,256]{3,2,1,0:T(8,128)} copy(f32[10,8,128,256]{3,1,2,0:T(8,128)S(1)} %bitcast.174) | data formatting | bytes 20971520 | tf_op jit(solution)/shard_map/while
  177.5 11.1 %bitcast_add_fusion.2 = f32[80,128,256]{2,1,0:T(8,128)} fusion(f32[10,8,128,256]{3,2,1,0:T(8,128)} %copy.87, f32[80,128,256]{2,1,0:T(8,128)} %get-tuple-element.279, pred[]{:T(512)S(6)} %compare.20), kind=kLoop, calls=%fused_computation.23.clone.1 | loop fusion | flops 5242880 | bytes 31457280 | tf_op jit(solution)/shard_map/while/body/eval_jaxpr/add | solution.py:97
  188.7 5.8 copy.84
  197.9 8.7 %fusion.140 = (bf16[8,8,128,256]{3,2,1,0:T(8,128)(2,1)}, bf16[8,8,128,256]{3,2,1,0:T(8,128)(2,1)}) fusion(bf16[4,8,128,256]{3,2,1,0:T(8,128)(2,1)S(1)} %get-tuple-element.292, s32[]{:T(128)} %get-tuple-element.278, bf16[8,8,128,256]{3,1,2,0:T(8,128)(2,1)} %bitcast.177, bf16[4,8,8,128,128]{3,4,2,1,0:T(8,128)(2,1)} %get-tuple-element.293), kind=kOutput, calls=%fused_computation.25.clone.1 | convolution fusion | flops 1085276160 | bytes 15730176 | tf_op jit(solution)/shard_map/while/body/eval_jaxpr/skab,sar->skbr/dot_general | solution.py:91
  222.0 7.1 %copy.87 = f32[10,8,128,256]{3,2,1,0:T(8,128)} copy(f32[10,8,128,256]{3,1,2,0:T(8,128)S(1)} %bitcast.174) | data formatting | bytes 20971520 | tf_op jit(solution)/shard_map/while
  229.1 14.1 %bitcast_add_fusion.2 = f32[80,128,256]{2,1,0:T(8,128)} fusion(f32[10,8,128,256]{3,2,1,0:T(8,128)} %copy.87, f32[80,128,256]{2,1,0:T(8,128)} %get-tuple-element.279, pred[]{:T(512)S(6)} %compare.20), kind=kLoop, calls=%fused_computation.23.clone.1 | loop fusion | flops 5242880 | bytes 31457280 | tf_op jit(solution)/shard_map/while/body/eval_jaxpr/add | solution.py:97
  252.4 8.7 %fusion.140 = (bf16[8,8,128,256]{3,2,1,0:T(8,128)(2,1)}, bf16[8,8,128,256]{3,2,1,0:T(8,128)(2,1)}) fusion(bf16[4,8,128,256]{3,2,1,0:T(8,128)(2,1)S(1)} %get-tuple-element.292, s32[]{:T(128)} %get-tuple-element.278, bf16[8,8,128,256]{3,1,2,0:T(8,128)(2,1)} %bitcast.177, bf16[4,8,8,128,128]{3,4,2,1,0:T(8,128)(2,1)} %get-tuple-element.293), kind=kOutput, calls=%fused_computation.25.clone.1 | convolution fusion | flops 1085276160 | bytes 15730176 | tf_op jit(solution)/shard_map/while/body/eval_jaxpr/skab,sar->skbr/dot_general | solution.py:91
  276.6 7.1 %copy.87 = f32[10,8,128,256]{3,2,1,0:T(8,128)} copy(f32[10,8,128,256]{3,1,2,0:T(8,128)S(1)} %bitcast.174) | data formatting | bytes 20971520 | tf_op jit(solution)/shard_map/while
  283.7 14.1 %bitcast_add_fusion.2 = f32[80,128,256]{2,1,0:T(8,128)} fusion(f32[10,8,128,256]{3,2,1,0:T(8,128)} %copy.87, f32[80,128,256]{2,1,0:T(8,128)} %get-tuple-element.279, pred[]{:T(512)S(6)} %compare.20), kind=kLoop, calls=%fused_computation.23.clone.1 | loop fusion | flops 5242880 | bytes 31457280 | tf_op jit(solution)/shard_map/while/body/eval_jaxpr/add | solution.py:97
  297.8 5.8 copy.84
  307.0 8.7 %fusion.140 = (bf16[8,8,128,256]{3,2,1,0:T(8,128)(2,1)}, bf16[8,8,128,256]{3,2,1,0:T(8,128)(2,1)}) fusion(bf16[4,8,128,256]{3,2,1,0:T(8,128)(2,1)S(1)} %get-tuple-element.292, s32[]{:T(128)} %get-tuple-element.278, bf16[8,8,128,256]{3,1,2,0:T(8,128)(2,1)} %bitcast.177, bf16[4,8,8,128,128]{3,4,2,1,0:T(8,128)(2,1)} %get-tuple-element.293), kind=kOutput, calls=%fused_computation.25.clone.1 | convolution fusion | flops 1085276160 | bytes 15730176 | tf_op jit(solution)/shard_map/while/body/eval_jaxpr/skab,sar->skbr/dot_general | solution.py:91
  331.2 7.1 %copy.87 = f32[10,8,128,256]{3,2,1,0:T(8,128)} copy(f32[10,8,128,256]{3,1,2,0:T(8,128)S(1)} %bitcast.174) | data formatting | bytes 20971520 | tf_op jit(solution)/shard_map/while
  338.2 14.1 %bitcast_add_fusion.2 = f32[80,128,256]{2,1,0:T(8,128)} fusion(f32[10,8,128,256]{3,2,1,0:T(8,128)} %copy.87, f32[80,128,256]{2,1,0:T(8,128)} %get-tuple-element.279, pred[]{:T(512)S(6)} %compare.20), kind=kLoop, calls=%fused_computation.23.clone.1 | loop fusion | flops 5242880 | bytes 31457280 | tf_op jit(solution)/shard_map/while/body/eval_jaxpr/add | solution.py:97
  352.3 7.0 %convert_element_type.99 = bf16[80,128,256]{2,1,0:T(8,128)(2,1)} convert(f32[80,128,256]{2,1,0:T(8,128)} %get-tuple-element.76) | non-fusion elementwise | flops 2621440 | bytes 15728640 | tf_op jit(solution)/shard_map/convert_element_type | solution.py:101
  359.4 77.8 %reduce-scatter.4.cloned.1.call-done = bf16[5,128,256]{2,1,0:T(8,128)(2,1)} async-done(((bf16[80,128,256]{2,1,0:T(8,128)(2,1)}), bf16[5,128,256]{2,1,0:T(8,128)(2,1)}) %reduce-scatter.4.cloned.1.call-update) | async-done | bytes 327696
  446.1 6.0 collective-permute-done
  471.9 9.0 %all-to-all-start = ((s32[8,1,4]{2,1,0:T(1,128)}), s32[8,1,4]{2,1,0:T(1,128)S(1)}, u32[]{:S(2)}, u32[]{:S(2)}) async-start(s32[8,1,4]{2,1,0:T(1,128)} %bitcast.10), calls=%async_computation | async-start | bytes 8192 | tf_op jit(solution)/shard_map/all_to_all | solution.py:120
  534.1 69.7 %while.21 = (s32[]{:T(128)}, bf16[4,8,128,256]{3,2,1,0:T(8,128)(2,1)}, s32[4,8,8]{2,1,0:T(8,128)S(1)}, bf16[80,128,256]{2,1,0:T(8,128)(2,1)}, bf16[4,8,128,256]{...) while((s32[]{:T(128)}, ...), condition=%wide.region_4.5_spmd, body=%wide.region_3.4_spmd.sunk | while | flops 1414796288 | bytes 31985052 | solution.py:114
  534.4 5.8 copy.82
  544.1 7.6 %fusion.130 = bf16[4,8,128,256]{3,2,1,0:T(8,128)(2,1)} fusion(bf16[4,8,128,256]{3,2,1,0:T(8,128)(2,1)} %get-tuple-element.305, s32[]{:T(128)} %get-tuple-element.304, bf16[8,8,128,256]{3,1,2,0:T(8,128)(2,1)} %bitcast.181, bf16[4,8,8,128,128]{3,4,2,1,0:T(8,128)(2,1)} %get-tuple-element.317, f32[8]{0:T(128)S(1)} %fusion.129, ...), kind=kOutput, calls=%fused_computation.12.clone.1 | convolution fusion | flops 1077149696 | bytes 12060672 | tf_op jit(solution)/shard_map/while/body/eval_jaxpr/skab,skbr->sar/dot_general | solution.py:109
  561.5 7.6 %fusion.130 = bf16[4,8,128,256]{3,2,1,0:T(8,128)(2,1)} fusion(bf16[4,8,128,256]{3,2,1,0:T(8,128)(2,1)} %get-tuple-element.305, s32[]{:T(128)} %get-tuple-element.304, bf16[8,8,128,256]{3,1,2,0:T(8,128)(2,1)} %bitcast.181, bf16[4,8,8,128,128]{3,4,2,1,0:T(8,128)(2,1)} %get-tuple-element.317, f32[8]{0:T(128)S(1)} %fusion.129, ...), kind=kOutput, calls=%fused_computation.12.clone.1 | convolution fusion | flops 1077149696 | bytes 12060672 | tf_op jit(solution)/shard_map/while/body/eval_jaxpr/skab,skbr->sar/dot_general | solution.py:109
  578.9 7.6 %fusion.130 = bf16[4,8,128,256]{3,2,1,0:T(8,128)(2,1)} fusion(bf16[4,8,128,256]{3,2,1,0:T(8,128)(2,1)} %get-tuple-element.305, s32[]{:T(128)} %get-tuple-element.304, bf16[8,8,128,256]{3,1,2,0:T(8,128)(2,1)} %bitcast.181, bf16[4,8,8,128,128]{3,4,2,1,0:T(8,128)(2,1)} %get-tuple-element.317, f32[8]{0:T(128)S(1)} %fusion.129, ...), kind=kOutput, calls=%fused_computation.12.clone.1 | convolution fusion | flops 1077149696 | bytes 12060672 | tf_op jit(solution)/shard_map/while/body/eval_jaxpr/skab,skbr->sar/dot_general | solution.py:109
  596.3 7.6 %fusion.130 = bf16[4,8,128,256]{3,2,1,0:T(8,128)(2,1)} fusion(bf16[4,8,128,256]{3,2,1,0:T(8,128)(2,1)} %get-tuple-element.305, s32[]{:T(128)} %get-tuple-element.304, bf16[8,8,128,256]{3,1,2,0:T(8,128)(2,1)} %bitcast.181, bf16[4,8,8,128,128]{3,4,2,1,0:T(8,128)(2,1)} %get-tuple-element.317, f32[8]{0:T(128)S(1)} %fusion.129, ...), kind=kOutput, calls=%fused_computation.12.clone.1 | convolution fusion | flops 1077149696 | bytes 12060672 | tf_op jit(solution)/shard_map/while/body/eval_jaxpr/skab,skbr->sar/dot_general | solution.py:109
  603.8 7.3 %all-to-all-start.1 = ((bf16[8,4,128,256]{3,2,1,0:T(8,128)(2,1)}), bf16[8,4,128,256]{3,2,1,0:T(8,128)(2,1)S(1)}, u32[]{:S(2)}, u32[]{:S(2)}) async-start(bf16[8,4,128,256]{3,2,1,0:T(8,128)(2,1)} %bitcast.192), calls=%async_computation.1 | async-start | bytes 4194304 | tf_op jit(solution)/shard_map/all_to_all | solution.py:117
  611.8 25.7 %all-to-all-done.1 = bf16[8,4,128,256]{3,2,1,0:T(8,128)(2,1)S(1)} async-done(((bf16[8,4,128,256]{3,2,1,0:T(8,128)(2,1)}), bf16[8,4,128,256]{3,2,1,0:T(8,128)(2,1)S(1)}, u32[]{:S(2)}, u32[]{:S(2)}) %all-to-all-start.1) | async-done | bytes 2097184 | tf_op jit(solution)/shard_map/all_to_all | solution.py:117
  (159 shorter events, 218.9 us)
Async XLA Ops:
  7.2 5.2 copy-start.9
  7.2 56.5 %all-gather.5.cloned.1.call-start = ((), (), s32[]{:S(2)}) async-start(), calls=%async_computation.4 | async-start | bytes 9437184 | tf_op jit(solution)/shard_map/all_gather | solution.py:63
  9.9 112.7 %all-gather.3.cloned.1.call-start = ((), (), s32[]{:S(2)}) async-start(), calls=%async_computation.3 | async-start | bytes 5570560 | tf_op jit(solution)/shard_map/all_gather | solution.py:66
  11.8 425.3 %reduce-scatter.4.cloned.1.call-start = ((), (), s32[]{:S(2)}) async-start(), calls=%async_computation.5 | async-start | bytes 5570560
  13.3 12.1 %copy-start.6 = (s32[32,8]{0,1:T(8,128)S(1)}, s32[32,8]{0,1:T(8,128)}, u32[]{:S(2)}) copy-start(s32[32,8]{0,1:T(8,128)} %param.12) | copy-start | bytes 3076
  13.3 12.1 %copy-start.7 = (s32[32]{0:T(128)S(1)}, s32[32]{0:T(128)}, u32[]{:S(2)}) copy-start(s32[32]{0:T(128)} %param.11) | copy-start | bytes 388
  159.8 2.2 copy-start
  211.3 2.2 copy-start
  265.9 2.2 copy-start
  359.4 80.8 %copy-start.2 = (f32[640,256]{1,0:T(8,128)S(1)}, f32[640,256]{1,0:T(8,128)}, u32[]{:S(2)}) copy-start(f32[640,256]{1,0:T(8,128)} %param.15) | copy-start | bytes 1966084
  359.4 111.8 %copy-start.8 = (s32[32]{0:T(128)S(1)}, s32[32]{0:T(128)}, u32[]{:S(2)}) copy-start(s32[32]{0:T(128)} %param.11) | copy-start | bytes 388
  437.2 3.0 copy-start.3
  441.3 10.8 %collective-permute-start = (bf16[5,128,256]{2,1,0:T(8,128)(2,1)S(1)}, bf16[5,128,256]{2,1,0:T(8,128)(2,1)S(1)}, u32[]{:S(2)}, u32[]{:S(2)}) collective-permute-start(bf16[5,128,256]{2,1,0:T(8,128)(2,1)S(1)} %get-tuple-element.173), channel_id=1, source_target_pairs={{0,1},{1,2},{2,3},{3,4},{4,5},{5,6},{6,7},{7,8},{8,9},{9,10},{10,1... | collective-permute-start | bytes 983048 | tf_op jit(solution)/shard_map/ppermute | solution.py:17
  442.3 9.8 %collective-permute-start.1 = (bf16[5,128,256]{2,1,0:T(8,128)(2,1)S(1)}, bf16[5,128,256]{2,1,0:T(8,128)(2,1)S(1)}, u32[]{:S(2)}, u32[]{:S(2)}) collective-permute-start(bf16[5,128,256]{2,1,0:T(8,128)(2,1)S(1)} %get-tuple-element.173), channel_id=1, source_target_pairs={{0,15},{1,0},{2,1},{3,2},{4,3},{5,4},{6,5},{7,6},{8,7},{9,8},{10,9... | collective-permute-start | bytes 983048 | tf_op jit(solution)/shard_map/ppermute | solution.py:20
  452.1 14.6 %copy-start.5 = (bf16[5,128,256]{2,1,0:T(8,128)(2,1)}, bf16[5,128,256]{2,1,0:T(8,128)(2,1)S(1)}, u32[]{:S(2)}) copy-start(bf16[5,128,256]{2,1,0:T(8,128)(2,1)S(1)} %collective-permute-done) | copy-start | bytes 983044
  452.1 9.8 %collective-permute-start.2 = (bf16[5,128,256]{2,1,0:T(8,128)(2,1)S(1)}, bf16[5,128,256]{2,1,0:T(8,128)(2,1)S(1)}, u32[]{:S(2)}, u32[]{:S(2)}) collective-permute-start(bf16[5,128,256]{2,1,0:T(8,128)(2,1)S(1)} %collective-permute-done), channel_id=1, source_target_pairs={{0,1},{1,2},{2,3},{3,4},{4,5},{5,6},{6,7},{7,8},{8,9},{9,10},{10,1... | collective-permute-start | bytes 983048 | tf_op jit(solution)/shard_map/ppermute | solution.py:17
  452.1 9.8 %copy-start.4 = (bf16[5,128,256]{2,1,0:T(8,128)(2,1)}, bf16[5,128,256]{2,1,0:T(8,128)(2,1)S(1)}, u32[]{:S(2)}) copy-start(bf16[5,128,256]{2,1,0:T(8,128)(2,1)S(1)} %collective-permute-done.1) | copy-start | bytes 983044
  452.1 9.8 %collective-permute-start.3 = (bf16[5,128,256]{2,1,0:T(8,128)(2,1)S(1)}, bf16[5,128,256]{2,1,0:T(8,128)(2,1)}, u32[]{:S(2)}, u32[]{:S(2)}) collective-permute-start(bf16[5,128,256]{2,1,0:T(8,128)(2,1)S(1)} %collective-permute-done.1), channel_id=1, source_target_pairs={{0,15},{1,0},{2,1},{3,2},{4,3},{5,4},{6,5},{7,6},{8,7},{9,8},{10,9... | collective-permute-start | bytes 983048 | tf_op jit(solution)/shard_map/ppermute | solution.py:20
  461.9 9.2 %collective-permute-start.4 = (bf16[5,128,256]{2,1,0:T(8,128)(2,1)S(1)}, bf16[5,128,256]{2,1,0:T(8,128)(2,1)S(1)}, u32[]{:S(2)}, u32[]{:S(2)}) collective-permute-start(bf16[5,128,256]{2,1,0:T(8,128)(2,1)S(1)} %collective-permute-done.2), channel_id=1, source_target_pairs={{0,1},{1,2},{2,3},{3,4},{4,5},{5,6},{6,7},{7,8},{8,9},{9,10},{10,1... | collective-permute-start | bytes 983048 | tf_op jit(solution)/shard_map/ppermute | solution.py:17
  461.9 20.7 %collective-permute-start.5 = (bf16[5,128,256]{2,1,0:T(8,128)(2,1)}, bf16[5,128,256]{2,1,0:T(8,128)(2,1)S(1)}, u32[]{:S(2)}, u32[]{:S(2)}) collective-permute-start(bf16[5,128,256]{2,1,0:T(8,128)(2,1)} %collective-permute-done.3), channel_id=1, source_target_pairs={{0,15},{1,0},{2,1},{3,2},{4,3},{5,4},{6,5},{7,6},{8,7},{9,8},{10,9... | collective-permute-start | bytes 983048 | tf_op jit(solution)/shard_map/ppermute | solution.py:20
  471.2 18.2 %collective-permute-start.6 = (bf16[5,128,256]{2,1,0:T(8,128)(2,1)S(1)}, bf16[5,128,256]{2,1,0:T(8,128)(2,1)S(1)}, u32[]{:S(2)}, u32[]{:S(2)}) collective-permute-start(bf16[5,128,256]{2,1,0:T(8,128)(2,1)S(1)} %collective-permute-done.4), channel_id=1, source_target_pairs={{0,1},{1,2},{2,3},{3,4},{4,5},{5,6},{6,7},{7,8},{8,9},{9,10},{10,1... | collective-permute-start | bytes 983048 | tf_op jit(solution)/shard_map/ppermute | solution.py:17
  471.9 132.0 %all-to-all-start = ((s32[8,1,4]{2,1,0:T(1,128)}), s32[8,1,4]{2,1,0:T(1,128)S(1)}, u32[]{:S(2)}, u32[]{:S(2)}) async-start(s32[8,1,4]{2,1,0:T(1,128)} %bitcast.10), calls=%async_computation | async-start | bytes 8192 | tf_op jit(solution)/shard_map/all_to_all | solution.py:120
  482.6 12.2 %collective-permute-start.7 = (bf16[5,128,256]{2,1,0:T(8,128)(2,1)S(1)}, bf16[5,128,256]{2,1,0:T(8,128)(2,1)S(1)}, u32[]{:S(2)}, u32[]{:S(2)}) collective-permute-start(bf16[5,128,256]{2,1,0:T(8,128)(2,1)S(1)} %collective-permute-done.5), channel_id=1, source_target_pairs={{0,15},{1,0},{2,1},{3,2},{4,3},{5,4},{6,5},{7,6},{8,7},{9,8},{10,9... | collective-permute-start | bytes 983048 | tf_op jit(solution)/shard_map/ppermute | solution.py:20
  489.4 12.3 %collective-permute-start.8 = (bf16[5,128,256]{2,1,0:T(8,128)(2,1)S(1)}, bf16[5,128,256]{2,1,0:T(8,128)(2,1)S(1)}, u32[]{:S(2)}, u32[]{:S(2)}) collective-permute-start(bf16[5,128,256]{2,1,0:T(8,128)(2,1)S(1)} %collective-permute-done.6), channel_id=1, source_target_pairs={{0,1},{1,2},{2,3},{3,4},{4,5},{5,6},{6,7},{7,8},{8,9},{9,10},{10,1... | collective-permute-start | bytes 983048 | tf_op jit(solution)/shard_map/ppermute | solution.py:17
  494.8 11.8 %collective-permute-start.9 = (bf16[5,128,256]{2,1,0:T(8,128)(2,1)S(1)}, bf16[5,128,256]{2,1,0:T(8,128)(2,1)S(1)}, u32[]{:S(2)}, u32[]{:S(2)}) collective-permute-start(bf16[5,128,256]{2,1,0:T(8,128)(2,1)S(1)} %collective-permute-done.7), channel_id=1, source_target_pairs={{0,15},{1,0},{2,1},{3,2},{4,3},{5,4},{6,5},{7,6},{8,7},{9,8},{10,9... | collective-permute-start | bytes 983048 | tf_op jit(solution)/shard_map/ppermute | solution.py:20
  501.8 11.4 %collective-permute-start.10 = (bf16[5,128,256]{2,1,0:T(8,128)(2,1)S(1)}, bf16[5,128,256]{2,1,0:T(8,128)(2,1)S(1)}, u32[]{:S(2)}, u32[]{:S(2)}) collective-permute-start(bf16[5,128,256]{2,1,0:T(8,128)(2,1)S(1)} %collective-permute-done.8), channel_id=1, source_target_pairs={{0,1},{1,2},{2,3},{3,4},{4,5},{5,6},{6,7},{7,8},{8,9},{9,10},{10,1... | collective-permute-start | bytes 983048 | tf_op jit(solution)/shard_map/ppermute | solution.py:17
  506.6 10.9 %collective-permute-start.11 = (bf16[5,128,256]{2,1,0:T(8,128)(2,1)S(1)}, bf16[5,128,256]{2,1,0:T(8,128)(2,1)S(1)}, u32[]{:S(2)}, u32[]{:S(2)}) collective-permute-start(bf16[5,128,256]{2,1,0:T(8,128)(2,1)S(1)} %collective-permute-done.9), channel_id=1, source_target_pairs={{0,15},{1,0},{2,1},{3,2},{4,3},{5,4},{6,5},{7,6},{8,7},{9,8},{10,9... | collective-permute-start | bytes 983048 | tf_op jit(solution)/shard_map/ppermute | solution.py:20
  513.2 10.6 %collective-permute-start.12 = (bf16[5,128,256]{2,1,0:T(8,128)(2,1)S(1)}, bf16[5,128,256]{2,1,0:T(8,128)(2,1)S(1)}, u32[]{:S(2)}, u32[]{:S(2)}) collective-permute-start(bf16[5,128,256]{2,1,0:T(8,128)(2,1)S(1)} %collective-permute-done.10), channel_id=1, source_target_pairs={{0,1},{1,2},{2,3},{3,4},{4,5},{5,6},{6,7},{7,8},{8,9},{9,10},{10,1... | collective-permute-start | bytes 983048 | tf_op jit(solution)/shard_map/ppermute | solution.py:17
  517.4 9.9 %collective-permute-start.13 = (bf16[5,128,256]{2,1,0:T(8,128)(2,1)S(1)}, bf16[5,128,256]{2,1,0:T(8,128)(2,1)S(1)}, u32[]{:S(2)}, u32[]{:S(2)}) collective-permute-start(bf16[5,128,256]{2,1,0:T(8,128)(2,1)S(1)} %collective-permute-done.11), channel_id=1, source_target_pairs={{0,15},{1,0},{2,1},{3,2},{4,3},{5,4},{6,5},{7,6},{8,7},{9,8},{10,9... | collective-permute-start | bytes 983048 | tf_op jit(solution)/shard_map/ppermute | solution.py:20
  523.7 9.6 %collective-permute-start.14 = (bf16[5,128,256]{2,1,0:T(8,128)(2,1)S(1)}, bf16[5,128,256]{2,1,0:T(8,128)(2,1)S(1)}, u32[]{:S(2)}, u32[]{:S(2)}) collective-permute-start(bf16[5,128,256]{2,1,0:T(8,128)(2,1)S(1)} %collective-permute-done.12), channel_id=1, source_target_pairs={{0,1},{1,2},{2,3},{3,4},{4,5},{5,6},{6,7},{7,8},{8,9},{9,10},{10,1... | collective-permute-start | bytes 983048 | tf_op jit(solution)/shard_map/ppermute | solution.py:17
  603.8 33.7 %all-to-all-start.1 = ((bf16[8,4,128,256]{3,2,1,0:T(8,128)(2,1)}), bf16[8,4,128,256]{3,2,1,0:T(8,128)(2,1)S(1)}, u32[]{:S(2)}, u32[]{:S(2)}) async-start(bf16[8,4,128,256]{3,2,1,0:T(8,128)(2,1)} %bitcast.192), calls=%async_computation.1 | async-start | bytes 4194304 | tf_op jit(solution)/shard_map/all_to_all | solution.py:117
  639.3 4.8 copy-start.1
  (1 other events, 2.2 us)
Sparse Core Ops, SparseCore 0:
  10.3 53.3 all-gather.4
  66.4 56.2 all-gather.2
  359.5 77.5 reduce-scatter.3
